TPU v7x, 32 devices: a whole 2x2x4 slice. The times are simulated.
32 devices in a mesh: rep: 2 (over x), pts: 16 (over z, y, core).
Axes of the slice: x: 2, y: 2, z: 4, core: 2. Of those that a mesh axis runs over, the one named last changes fastest.
Arguments:
- orbitals: bfloat16 [64, 32, 512], P(('rep', 'pts')), parts along dimension 0, may hold values from -6 to 6
- points: bfloat16 [12288, 512], P('pts'), may hold values from -0.25 to 0.25
- coupling: bfloat16 [12288, 4096], P('pts'), may hold values from -0.01953125 to 0.01953125
- fields: int32 [64, 4096], P('rep'), parts along dimension 0, may hold values from 0 to 3
- destination: int32 [64], P('rep'), parts along dimension 0, may hold values from 0 to 15, as said below
Outputs:
- moved: bfloat16 [96, 32, 512], P(('rep', 'pts')), parts along dimension 0
There are 2 independent parts, one for each index of `rep`. A program takes and returns all parts, laid end to end along the dimension named above; an argument that names none is the same for every part. Nothing has to cross between parts.
Inputs may be any that keep to these rules, and one draw needn't show every extreme that they name: Each group is the destination of at most 3 walkers; some group receives exactly 3, and the 2 walkers of some group all go to it.
All inputs are finite; a program needn't handle non-finite values.
Results may differ from a plain program's by a relative error of at most 0.008.
Values may be sent and summed in bfloat16 or wider, within the bound.
A program may use at most 64 MiB of HBM per device.

v0:
```python
import jax
import jax.numpy as jnp
from jax import lax
from jax.sharding import PartitionSpec as P

LEVELS = (-2.3344142183389773, -0.7419637843027258, 0.7419637843027258, 2.3344142183389773)


def field_values(fields):
    values = jnp.zeros(fields.shape, jnp.float32)
    for level_index in range(4):
        values = values + jnp.where(fields == level_index, LEVELS[level_index], 0.0)
    return values.astype(jnp.bfloat16)


def rotate(block):
    half_rows = block.shape[-2] // 2
    return jnp.concatenate([-block[..., half_rows:, :], block[..., :half_rows, :]], axis=-2)


def arrival_targets(destination, slot_count):
    walker_ids = jnp.arange(destination.shape[0], dtype=jnp.int32)
    earlier = (destination[:, None] == destination[None, :]) & (
        walker_ids[None, :] < walker_ids[:, None]
    )
    return destination * slot_count + jnp.sum(earlier.astype(jnp.int32), axis=1)


def pack_sends(propagated, destination, position, group_count):
    own_count = propagated.shape[0]
    own_dest = lax.dynamic_slice_in_dim(destination, position * own_count, own_count)
    group_ids = jnp.arange(group_count, dtype=jnp.int32)
    onehot = (own_dest[None, :] == group_ids[:, None]).astype(jnp.bfloat16)
    return onehot[:, :, None, None] * propagated[None]


def place_rows(rows_all, targets, position, slot_count):
    flattened = rows_all.reshape(rows_all.shape[0], -1)
    slot_ids = position * slot_count + jnp.arange(slot_count, dtype=jnp.int32)
    selector = (targets[None, :] == slot_ids[:, None]).astype(jnp.bfloat16)
    placed = jnp.dot(selector, flattened, preferred_element_type=jnp.float32).astype(jnp.bfloat16)
    return placed.reshape((slot_count,) + rows_all.shape[1:])


def migrate(propagated, destination, targets, position, group_count, slot_count):
    sends = pack_sends(propagated, destination, position, group_count)
    received = lax.all_to_all(sends, "pts", split_axis=0, concat_axis=0, tiled=True)
    merged = received.reshape((received.shape[0] * received.shape[1],) + received.shape[2:])
    return place_rows(merged, targets, position, slot_count)


def per_device(orbitals, points, coupling, fields, destination):
    own_count = orbitals.shape[0]
    slot_count = own_count + own_count // 2
    position = lax.axis_index("pts")
    group_count = lax.axis_size("pts")
    targets = arrival_targets(destination, slot_count)
    values = field_values(fields)
    weights_here = jnp.einsum("wg,pg->wp", values, coupling, preferred_element_type=jnp.float32)
    spread = lax.all_to_all(weights_here, "pts", split_axis=0, concat_axis=1, tiled=True)
    table = lax.all_gather(points, "pts", axis=0, tiled=True)

    def local_apply(rows):
        inner = jnp.einsum("wrn,pn->wrp", rows, table, preferred_element_type=jnp.float32)
        scaled = (inner * spread[:, None, :]).astype(jnp.bfloat16)
        return rotate(jnp.einsum("wrp,pn->wrn", scaled, table, preferred_element_type=jnp.float32))

    first = local_apply(orbitals)
    second = 0.5 * local_apply(first.astype(jnp.bfloat16))
    propagated = (orbitals.astype(jnp.float32) + first + second).astype(jnp.bfloat16)
    return migrate(propagated, destination, targets, position, group_count, slot_count)


def solution(mesh):
    return jax.shard_map(
        per_device,
        mesh=mesh,
        in_specs=(
            P(("rep", "pts"), None, None),
            P("pts", None),
            P("pts", None),
            P("rep", None),
            P("rep"),
        ),
        out_specs=P(("rep", "pts"), None, None),
        check_vma=False,
    )
```

profile of v0, /device:TPU:1, one launch (start us, length us, event | category | flops | bytes accessed | tf_op | source)
XLA Modules:
  0.0 179.4 jit_solution(3259843512029514543)
XLA Ops:
  6.5 0.0 copy-start.1
  6.5 0.0 copy-start
  6.5 0.0 all-gather.2.cloned.1.call-start
  6.5 0.7 all-gather.2.cloned.1.call-update
  7.3 4.9 %fusion.14 = f32[32,768]{1,0:T(8,128)S(1)} fusion(bf16[768,4096]{1,0:T(8,128)(2,1)} %param.7, s32[32,4096]{1,0:T(8,128)} %param.8), kind=kOutput, calls=%fused_computation.15 | convolution fusion | flops 202899456 | bytes 6914048 | tf_op jit(solution)/shard_map/wg,pg->wp/dot_general | solution.py:59
  12.2 0.7 all_to_all.15
  12.9 7.3 %all-to-all-start = ((f32[16,2,768]{2,1,0:T(2,128)}), f32[16,2,768]{2,1,0:T(2,128)S(1)}, u32[]{:S(2)}, u32[]{:S(2)}) async-start(f32[16,2,768]{2,1,0:T(2,128)} %all_to_all.15), calls=%async_computation | async-start | bytes 196608 | tf_op jit(solution)/shard_map/all_to_all | solution.py:60
  20.2 0.0 copy-done.1
  20.2 0.1 dynamic_slice.3
  20.3 7.7 %all-to-all-done = f32[16,2,768]{2,1,0:T(2,128)S(1)} async-done(((f32[16,2,768]{2,1,0:T(2,128)}), f32[16,2,768]{2,1,0:T(2,128)S(1)}, u32[]{:S(2)}, u32[]{:S(2)}) %all-to-all-start) | async-done | bytes 98336 | tf_op jit(solution)/shard_map/all_to_all | solution.py:60
  28.0 86.4 %all-gather.2.cloned.1.call-done = bf16[12288,512]{1,0:T(8,128)(2,1)} async-done(((bf16[768,512]{1,0:T(8,128)(2,1)}), bf16[12288,512]{1,0:T(8,128)(2,1)}) %all-gather.2.cloned.1.call-update) | async-done | bytes 12582928 | tf_op jit(solution)/shard_map/all_gather | solution.py:61
  114.4 0.0 copy-done
  114.4 14.2 %fusion.5 = f32[2,32,512]{2,1,0:T(8,128)S(1)} fusion(bf16[12288,512]{1,0:T(8,128)(2,1)} %all-gather.2.cloned.1.call-done, bf16[2,32,512]{2,1,0:T(8,128)(2,1)S(1)} %copy-done, f32[2,12288]{1,0:T(2,128)S(1)} %bitcast.28), kind=kOutput, calls=%fused_computation.8 | convolution fusion | flops 1612185600 | bytes 12877824 | tf_op jit(solution)/shard_map/wrp,pn->wrn/dot_general | solution.py:66
  128.6 14.2 %fusion.2 = f32[2,32,512]{2,1,0:T(8,128)S(1)} fusion(bf16[12288,512]{1,0:T(8,128)(2,1)} %all-gather.2.cloned.1.call-done, f32[2,12288]{1,0:T(2,128)S(1)} %bitcast.29, f32[2,16,512]{2,1,0:T(8,128)S(1)} %get-tuple-element.8, f32[2,16,512]{2,1,0:T(8,128)S(1)} %get-tuple-element.7), kind=kOutput, calls=%fused_computation.5 | convolution fusion | flops 1612316672 | bytes 12943360 | tf_op jit(solution)/shard_map/wrp,pn->wrn/dot_general | solution.py:66
  142.9 1.1 broadcast_multiply_fusion
  144.0 3.7 %all-to-all-start.1 = ((bf16[16,2,32,512]{3,2,1,0:T(8,128)(2,1)}), bf16[16,2,32,512]{3,2,1,0:T(8,128)(2,1)S(1)}, u32[]{:S(2)}, u32[]{:S(2)}) async-start(bf16[16,2,32,512]{3,2,1,0:T(8,128)(2,1)} %broadcast_multiply_fusion), calls=%async_computation.1 | async-start | bytes 2097152 | tf_op jit(solution)/shard_map/all_to_all | solution.py:47
  147.7 0.2 convert_reduce_fusion
  147.9 23.0 %all-to-all-done.1 = bf16[16,2,32,512]{3,2,1,0:T(8,128)(2,1)S(1)} async-done(((bf16[16,2,32,512]{3,2,1,0:T(8,128)(2,1)}), bf16[16,2,32,512]{3,2,1,0:T(8,128)(2,1)S(1)}, u32[]{:S(2)}, u32[]{:S(2)}) %all-to-all-start.1) | async-done | bytes 1048608 | tf_op jit(solution)/shard_map/all_to_all | solution.py:47
  171.0 0.6 copy.6
  171.6 0.3 convolution_convert_fusion
  171.9 0.7 copy.9
  (6 shorter events, 0.1 us)
Async XLA Ops:
  6.5 13.7 %copy-start.1 = (s32[32]{0:T(128)S(1)}, s32[32]{0:T(128)}, u32[]{:S(2)}) copy-start(s32[32]{0:T(128)} %param.9) | copy-start | bytes 388
  6.5 107.8 %copy-start = (bf16[2,32,512]{2,1,0:T(8,128)(2,1)S(1)}, bf16[2,32,512]{2,1,0:T(8,128)(2,1)}, u32[]{:S(2)}) copy-start(bf16[2,32,512]{2,1,0:T(8,128)(2,1)} %param.5) | copy-start | bytes 196612
  6.5 107.8 %all-gather.2.cloned.1.call-start = ((), (), s32[]{:S(2)}) async-start(), calls=%async_computation.2 | async-start | bytes 13369344 | tf_op jit(solution)/shard_map/all_gather | solution.py:61
  12.9 15.1 %all-to-all-start = ((f32[16,2,768]{2,1,0:T(2,128)}), f32[16,2,768]{2,1,0:T(2,128)S(1)}, u32[]{:S(2)}, u32[]{:S(2)}) async-start(f32[16,2,768]{2,1,0:T(2,128)} %all_to_all.15), calls=%async_computation | async-start | bytes 196608 | tf_op jit(solution)/shard_map/all_to_all | solution.py:60
  144.0 26.9 %all-to-all-start.1 = ((bf16[16,2,32,512]{3,2,1,0:T(8,128)(2,1)}), bf16[16,2,32,512]{3,2,1,0:T(8,128)(2,1)S(1)}, u32[]{:S(2)}, u32[]{:S(2)}) async-start(bf16[16,2,32,512]{3,2,1,0:T(8,128)(2,1)} %broadcast_multiply_fusion), calls=%async_computation.1 | async-start | bytes 2097152 | tf_op jit(solution)/shard_map/all_to_all | solution.py:47
Sparse Core Ops, SparseCore 0:
  9.6 104.7 all-gather.1
where the time goes:
time: 181 us; the launch traced here: 179 us
  waiting for transfers between devices  118 us (65%)
  matrix products  33.7 us (19%)
  between operations  13.4 us (7%)
  starting transfers between devices  11 us (6%)
  local copies, waits for them, and re-layouts  2.05 us (1%)
    all_gather x1, waiting for transfers between devices, per_device(): table = lax.all_gather(points, 'pts', axis=0, tiled=True)  86.4 us
    dot_general x2, matrix products, local_apply(): jnp.einsum('wrp,pn->wrn', scaled, table, preferred_element_type=jnp.float32)  28.4 us
    all_to_all x1, waiting for transfers between devices, migrate(): lax.all_to_all(sends, 'pts', split_axis=0, concat_axis=0, tiled=True)  23 us
    all_to_all x1, waiting for transfers between devices, per_device(): lax.all_to_all(weights_here, 'pts', split_axis=0, concat_axis=1, tiled=True)  7.69 us
    all_to_all x1, starting transfers between devices, per_device(): lax.all_to_all(weights_here, 'pts', split_axis=0, concat_axis=1, tiled=True)  7.34 us
    dot_general x1, matrix products, per_device(): jnp.einsum('wg,pg->wp', values, coupling, preferred_element_type=jnp.floa...  4.92 us
    all_to_all x1, starting transfers between devices, migrate(): lax.all_to_all(sends, 'pts', split_axis=0, concat_axis=0, tiled=True)  3.7 us
  transfers between devices with their start and end apart: 3, of which 3 were waited for; matrix products, arithmetic and copies ran while one was open for 3% of the time, Pallas kernels for 0%

commit v1 on v0

v1 whole, which is shorter than its diff:
```python
import jax
import jax.numpy as jnp
from jax import lax
from jax.sharding import PartitionSpec as P

LEVELS = (-2.3344142183389773, -0.7419637843027258, 0.7419637843027258, 2.3344142183389773)


def field_values(fields):
    values = jnp.zeros(fields.shape, jnp.float32)
    for level_index in range(4):
        values = values + jnp.where(fields == level_index, LEVELS[level_index], 0.0)
    return values.astype(jnp.bfloat16)


def rotate(block):
    half_rows = block.shape[-2] // 2
    return jnp.concatenate([-block[..., half_rows:, :], block[..., :half_rows, :]], axis=-2)


def arrival_targets(destination, slot_count):
    walker_ids = jnp.arange(destination.shape[0], dtype=jnp.int32)
    earlier = (destination[:, None] == destination[None, :]) & (
        walker_ids[None, :] < walker_ids[:, None]
    )
    return destination * slot_count + jnp.sum(earlier.astype(jnp.int32), axis=1)


def place_rows(rows_all, targets, position, slot_count):
    flattened = rows_all.reshape(rows_all.shape[0], -1)
    slot_ids = position * slot_count + jnp.arange(slot_count, dtype=jnp.int32)
    selector = (targets[None, :] == slot_ids[:, None]).astype(jnp.bfloat16)
    placed = jnp.dot(selector, flattened, preferred_element_type=jnp.float32).astype(jnp.bfloat16)
    return placed.reshape((slot_count,) + rows_all.shape[1:])


def per_device(orbitals, points, coupling, fields, destination):
    own_count = orbitals.shape[0]
    slot_count = own_count + own_count // 2
    position = lax.axis_index("pts")
    targets = arrival_targets(destination, slot_count)
    values = field_values(fields)
    scale = jnp.einsum("wg,pg->wp", values, coupling, preferred_element_type=jnp.float32)

    def apply(rows):
        gathered = lax.all_gather(rows, "pts", axis=0, tiled=True)
        inner = jnp.einsum("wrn,pn->wrp", gathered, points, preferred_element_type=jnp.float32)
        scaled = (inner * scale[:, None, :]).astype(jnp.bfloat16)
        partial = jnp.einsum("wrp,pn->wrn", scaled, points, preferred_element_type=jnp.float32)
        return rotate(
            lax.psum_scatter(partial.astype(jnp.bfloat16), "pts", scatter_dimension=0, tiled=True).astype(jnp.float32)
        )

    first = apply(orbitals)
    second = 0.5 * apply(first.astype(jnp.bfloat16))
    propagated = (orbitals.astype(jnp.float32) + first + second).astype(jnp.bfloat16)
    everyone = lax.all_gather(propagated, "pts", axis=0, tiled=True)
    return place_rows(everyone, targets, position, slot_count)


def solution(mesh):
    return jax.shard_map(
        per_device,
        mesh=mesh,
        in_specs=(
            P(("rep", "pts"), None, None),
            P("pts", None),
            P("pts", None),
            P("rep", None),
            P("rep"),
        ),
        out_specs=P(("rep", "pts"), None, None),
        check_vma=False,
    )
```

time: 181 us -> 260 us (1.44)
  waiting for transfers between devices: 118 us -> 226 us
  matrix products: 33.7 us -> 13.3 us
  starting transfers between devices: 11 us -> 0.17 us
    reduce_scatter x0 -> x2, waiting for transfers between devices: none -> 109 us  [apply(): lax.psum_scatter(partial.astype(jnp.bfloat16), 'pts', scatter_dimension=0...]
    all_to_all x2 -> x0, waiting for transfers between devices: 30.7 us -> none  [the longest x1 23 us: migrate(): lax.all_to_all(sends, 'pts', split_axis=0, concat_axis=0, tiled=True)]
    all_gather x1 -> x3, waiting for transfers between devices: 86.4 us -> 116 us  [the longest x2 76.8 us: apply(): gathered = lax.all_gather(rows, 'pts', axis=0, tiled=True)]
    dot_general x2, matrix products: 28.4 us -> 8.03 us  [apply(): jnp.einsum('wrp,pn->wrn', scaled, points, preferred_element_type=jnp.floa...]
    all_to_all x2 -> x0, starting transfers between devices: 11 us -> none  [the longest x1 7.34 us: per_device(): lax.all_to_all(weights_here, 'pts', split_axis=0, concat_axis=1, tiled=True)]
  transfers between devices with their start and end apart: 3 -> 5, of which waited for: 3 -> 5; matrix products, arithmetic and copies ran while one was open for 3% -> 2% of each run, Pallas kernels for 0% -> 0%
where the time goes in v1:
time: 260 us; the launch traced here: 259 us
  waiting for transfers between devices  226 us (87%)
  matrix products  13.3 us (5%)
  between operations  13.2 us (5%)
  local copies, waits for them, and re-layouts  4.03 us (2%)
  other arithmetic  3.2 us (1%)
    reduce_scatter x2, waiting for transfers between devices, apply(): lax.psum_scatter(partial.astype(jnp.bfloat16), 'pts', scatter_dimension=0...  109 us
    all_gather x2, waiting for transfers between devices, apply(): gathered = lax.all_gather(rows, 'pts', axis=0, tiled=True)  76.8 us
    all_gather x1, waiting for transfers between devices, per_device(): everyone = lax.all_gather(propagated, 'pts', axis=0, tiled=True)  39.1 us
    dot_general x2, matrix products, apply(): jnp.einsum('wrp,pn->wrn', scaled, points, preferred_element_type=jnp.floa...  8.03 us
  transfers between devices with their start and end apart: 5, of which 5 were waited for; matrix products, arithmetic and copies ran while one was open for 2% of the time, Pallas kernels for 0%

profile of v1, /device:TPU:1, one launch (start us, length us, event | category | flops | bytes accessed | tf_op | source)
XLA Modules:
  0.0 259.4 jit_solution(14897041343639136582)
XLA Ops:
  6.5 0.0 copy-start
  6.5 0.0 all-gather.4.cloned.1.call-start
  6.5 0.7 all-gather.4.cloned.1.call-update
  7.3 0.0 reduce-scatter.3.cloned.1.call-start
  7.3 4.9 %fusion.4 = f32[32,768]{1,0:T(8,128)S(1)} fusion(bf16[768,4096]{1,0:T(8,128)(2,1)} %param.7, s32[32,4096]{1,0:T(8,128)} %param.8), kind=kOutput, calls=%fused_computation.8 | convolution fusion | flops 202899456 | bytes 6914048 | tf_op jit(solution)/shard_map/wg,pg->wp/dot_general | solution.py:43
  12.2 37.6 %all-gather.4.cloned.1.call-done = bf16[32,32,512]{2,1,0:T(8,128)(2,1)} async-done(((bf16[2,32,512]{2,1,0:T(8,128)(2,1)}), bf16[32,32,512]{2,1,0:T(8,128)(2,1)}) %all-gather.4.cloned.1.call-update) | async-done | bytes 1048592 | tf_op jit(solution)/shard_map/all_gather | solution.py:46
  49.8 0.0 copy-done
  49.9 4.0 %convolution_convert_fusion.2 = bf16[32,32,512]{2,1,0:T(8,128)(2,1)} fusion(bf16[32,32,512]{2,1,0:T(8,128)(2,1)} %all-gather.4.cloned.1.call-done, f32[32,768]{1,0:T(8,128)S(1)} %fusion.4, bf16[768,512]{1,0:T(8,128)(2,1)S(1)} %copy-done), kind=kOutput, calls=%fused_computation.4 | convolution fusion | flops 1612709888 | bytes 2981888 | tf_op jit(solution)/shard_map/wrp,pn->wrn/dot_general | solution.py:49
  53.9 0.0 reduce-scatter.3.cloned.1.call-update
  53.9 0.0 all-gather.6.cloned.1.call-start
  53.9 54.4 %reduce-scatter.3.cloned.1.call-done = bf16[2,32,512]{2,1,0:T(8,128)(2,1)} async-done(((bf16[32,32,512]{2,1,0:T(8,128)(2,1)}), bf16[2,32,512]{2,1,0:T(8,128)(2,1)}) %reduce-scatter.3.cloned.1.call-update) | async-done | bytes 65552 | tf_op jit(solution)/shard_map/reduce_scatter | solution.py:51
  108.4 0.8 convert_element_type.42
  109.3 0.8 slice.17
  110.0 0.6 fusion.16
  110.7 0.0 all-gather.6.cloned.1.call-update
  110.7 0.0 copy-start.1
  110.7 0.0 copy-start.2
  110.7 0.0 reduce-scatter.5.cloned.1.call-start
  110.8 39.2 %all-gather.6.cloned.1.call-done = bf16[32,32,512]{2,1,0:T(8,128)(2,1)} async-done(((bf16[2,32,512]{2,1,0:T(8,128)(2,1)}), bf16[32,32,512]{2,1,0:T(8,128)(2,1)}) %all-gather.6.cloned.1.call-update) | async-done | bytes 1048592 | tf_op jit(solution)/shard_map/all_gather | solution.py:46
  149.9 4.0 %convolution_convert_fusion.1 = bf16[32,32,512]{2,1,0:T(8,128)(2,1)} fusion(bf16[32,32,512]{2,1,0:T(8,128)(2,1)} %all-gather.6.cloned.1.call-done, f32[32,768]{1,0:T(8,128)S(1)} %fusion.4, bf16[768,512]{1,0:T(8,128)(2,1)S(1)} %copy-done), kind=kOutput, calls=%fused_computation.3 | convolution fusion | flops 1612709888 | bytes 2981888 | tf_op jit(solution)/shard_map/wrp,pn->wrn/dot_general | solution.py:49
  153.9 0.0 reduce-scatter.5.cloned.1.call-update
  154.0 0.0 all-gather.8.cloned.1.call-start
  154.0 54.4 %reduce-scatter.5.cloned.1.call-done = bf16[2,32,512]{2,1,0:T(8,128)(2,1)} async-done(((bf16[32,32,512]{2,1,0:T(8,128)(2,1)}), bf16[2,32,512]{2,1,0:T(8,128)(2,1)}) %reduce-scatter.5.cloned.1.call-update) | async-done | bytes 65552 | tf_op jit(solution)/shard_map/reduce_scatter | solution.py:51
  208.4 0.8 convert_element_type.46
  209.3 0.8 slice.19
  210.1 0.7 fusion.15
  210.7 0.0 all-gather.8.cloned.1.call-update
  210.8 0.2 convert_reduce_fusion
  211.0 39.1 %all-gather.8.cloned.1.call-done = bf16[32,32,512]{2,1,0:T(8,128)(2,1)} async-done(((bf16[2,32,512]{2,1,0:T(8,128)(2,1)}), bf16[32,32,512]{2,1,0:T(8,128)(2,1)}) %all-gather.8.cloned.1.call-update) | async-done | bytes 1048592 | tf_op jit(solution)/shard_map/all_gather | solution.py:57
  250.0 1.8 copy.6
  251.8 0.3 convolution_convert_fusion
  252.2 0.7 copy.9
  (6 shorter events, 0.0 us)
Async XLA Ops:
  6.5 43.3 %copy-start = (bf16[768,512]{1,0:T(8,128)(2,1)S(1)}, bf16[768,512]{1,0:T(8,128)(2,1)}, u32[]{:S(2)}) copy-start(bf16[768,512]{1,0:T(8,128)(2,1)} %param.6) | copy-start | bytes 2359300
  6.5 43.3 %all-gather.4.cloned.1.call-start = ((), (), s32[]{:S(2)}) async-start(), calls=%async_computation.2 | async-start | bytes 1114112 | tf_op jit(solution)/shard_map/all_gather | solution.py:46
  7.3 101.1 %reduce-scatter.3.cloned.1.call-start = ((), (), s32[]{:S(2)}) async-start(), calls=%async_computation.3 | async-start | bytes 1114112 | tf_op jit(solution)/shard_map/reduce_scatter | solution.py:51
  53.9 96.0 %all-gather.6.cloned.1.call-start = ((), (), s32[]{:S(2)}) async-start(), calls=%async_computation.4 | async-start | bytes 1114112 | tf_op jit(solution)/shard_map/all_gather | solution.py:46
  110.7 99.4 %copy-start.1 = (bf16[2,32,512]{2,1,0:T(8,128)(2,1)S(1)}, bf16[2,32,512]{2,1,0:T(8,128)(2,1)}, u32[]{:S(2)}) copy-start(bf16[2,32,512]{2,1,0:T(8,128)(2,1)} %param.5) | copy-start | bytes 196612
  110.7 100.1 %copy-start.2 = (s32[32]{0:T(128)S(1)}, s32[32]{0:T(128)}, u32[]{:S(2)}) copy-start(s32[32]{0:T(128)} %param.9) | copy-start | bytes 388
  110.7 97.7 %reduce-scatter.5.cloned.1.call-start = ((), (), s32[]{:S(2)}) async-start(), calls=%async_computation.5 | async-start | bytes 1114112 | tf_op jit(solution)/shard_map/reduce_scatter | solution.py:51
  154.0 96.1 %all-gather.8.cloned.1.call-start = ((), (), s32[]{:S(2)}) async-start(), calls=%async_computation.6 | async-start | bytes 1114112 | tf_op jit(solution)/shard_map/all_gather | solution.py:57
Sparse Core Ops, SparseCore 0:
  9.5 40.3 all-gather.3
  54.0 54.3 reduce-scatter.2
  110.8 39.0 all-gather.5
  154.1 54.3 reduce-scatter.4
  210.9 39.1 all-gather.7
